TPU v7x, 32 devices: a whole 2x2x4 slice. The times are simulated.
32 devices in a mesh: dom: 16 (over z, y, x), feat: 2 (over core).
Axes of the slice: x: 2, y: 2, z: 4, core: 2. Of those that a mesh axis runs over, the one named last changes fastest.
Arguments:
- features: bfloat16 [16384, 512], P('dom', 'feat'), may hold values from -6 to 6
- grad_out: bfloat16 [16384, 512], P('dom', 'feat'), may hold values from -6 to 6
- pre_act: bfloat16 [16384, 512], P('dom', 'feat'), may hold values from -6 to 6
- neigh_mean: bfloat16 [16384, 512], P('dom', 'feat'), may hold values from -6 to 6
- w_self: bfloat16 [512, 512], P('feat'), may hold values from -0.25 to 0.25
- w_neigh: bfloat16 [512, 512], P('feat'), may hold values from -0.25 to 0.25
- edge_from: int32 [131072], P('dom'), may hold values from 0 to 1535
- edge_to: int32 [131072], P('dom'), may hold values from 0 to 1535
- edge_count: int32 [16], P('dom'), may hold values from 2048 to 8192, as said below
- mirror_master: int32 [8192], P('dom'), may hold values from 0 to 63
- degrees: int32 [16384], P('dom'), may hold values from 1 to 16
Outputs:
- input_grad: bfloat16 [16384, 512], P('dom', 'feat')
- self_weight_grad: float32 [512, 512], P('feat')
- neigh_weight_grad: float32 [512, 512], P('feat')
Inputs may be any that keep to these rules, and one draw needn't show every extreme that they name: `edge_count`: equals 8192 in at least one partition.
All inputs are finite; a program needn't handle non-finite values.
Results may differ from a plain program's by a relative error of at most 0.0044.
Values may be sent and summed in bfloat16 or wider, within the bound.
A program may use at most 64 MiB of HBM per device.

v0:
```python
import jax
import jax.numpy as jnp
from jax import lax
from jax.sharding import PartitionSpec as P


def on_device(
    features,
    grad_out,
    pre_act,
    neigh_mean,
    w_self,
    w_neigh,
    edge_from,
    edge_to,
    edge_count,
    mirror_master,
    degrees,
):
    masters = features.shape[0]
    width_loc = features.shape[1]
    parts = lax.axis_size("dom")
    mirror_count = mirror_master.shape[0]
    slots = mirror_count // parts
    grad_pre = (grad_out.astype(jnp.float32) * (pre_act > 0).astype(jnp.float32)).astype(
        jnp.bfloat16
    )
    wanted = mirror_master.reshape(parts, slots)
    asked = lax.all_to_all(wanted, "dom", split_axis=0, concat_axis=0, tiled=True)
    block_cols = lax.all_gather(grad_pre, "feat", axis=1, tiled=True)
    contract = (((1,), (1,)), ((), ()))
    self_sum = lax.dot_general(block_cols, w_self, contract, preferred_element_type=jnp.float32)
    neigh_sum = lax.dot_general(block_cols, w_neigh, contract, preferred_element_type=jnp.float32)
    over_rows = (((0,), (0,)), ((), ()))
    grad_self = lax.dot_general(features, block_cols, over_rows, preferred_element_type=jnp.float32)
    grad_neigh = lax.dot_general(
        neigh_mean, block_cols, over_rows, preferred_element_type=jnp.float32
    )
    self_part, neigh_part, grad_self, grad_neigh = (self_sum, neigh_sum, grad_self, grad_neigh)
    scaled = (neigh_part / degrees[:, None].astype(jnp.float32)).astype(jnp.bfloat16)
    replies = scaled[asked.reshape(-1)].reshape(parts, slots, width_loc)
    mirror_rows = lax.all_to_all(replies, "dom", split_axis=0, concat_axis=0, tiled=True).reshape(
        mirror_count, width_loc
    )
    tables = jnp.concatenate([scaled, mirror_rows], axis=0)
    local_rows = tables.shape[0]
    edges = edge_from.shape[0]
    block_len = min(edges, 4096)
    blocks = edges // block_len
    positions = jnp.arange(edges, dtype=jnp.int32).reshape(blocks, block_len)
    limit = edge_count[0]

    def add_block(summed, pieces):
        sources, sinks, places = pieces
        is_live = places < limit
        contrib = jnp.where(is_live[:, None], tables[sinks].astype(jnp.float32), jnp.float32(0.0))
        return (summed.at[sources].add(contrib), None)

    summed, unused = lax.scan(
        add_block,
        jnp.zeros((local_rows, width_loc), jnp.float32),
        (edge_from.reshape(blocks, block_len), edge_to.reshape(blocks, block_len), positions),
    )
    mirror_grad = summed[masters:].astype(jnp.bfloat16)
    returned = lax.all_to_all(
        mirror_grad.reshape(parts, slots, width_loc), "dom", split_axis=0, concat_axis=0, tiled=True
    )
    master_add = jax.ops.segment_sum(
        returned.reshape(mirror_count, width_loc).astype(jnp.float32),
        asked.reshape(-1),
        num_segments=masters,
    )
    input_grad = (self_part + summed[:masters] + master_add).astype(jnp.bfloat16)
    self_weight_grad, neigh_weight_grad = lax.psum((grad_self, grad_neigh), "dom")
    return (input_grad, self_weight_grad, neigh_weight_grad)


def solution(mesh):
    placed = (
        P("dom", "feat"),
        P("dom", "feat"),
        P("dom", "feat"),
        P("dom", "feat"),
        P("feat", None),
        P("feat", None),
        P("dom"),
        P("dom"),
        P("dom"),
        P("dom"),
        P("dom"),
    )
    return jax.shard_map(
        on_device,
        mesh=mesh,
        in_specs=placed,
        out_specs=(P("dom", "feat"), P("feat", None), P("feat", None)),
        check_vma=False,
    )
```

profile of v0, /device:TPU:0, one launch (start us, length us, event | category | flops | bytes accessed | tf_op | source)
XLA Modules:
  0.0 166.6 jit_solution(8681521545837876625)
XLA Ops:
  7.2 0.0 all-gather.2.cloned.1.call-start
  7.3 2.2 %select_convert_fusion = bf16[1024,256]{1,0:T(8,128)(2,1)} fusion(bf16[1024,256]{1,0:T(8,128)(2,1)} %param.14, bf16[1024,256]{1,0:T(8,128)(2,1)} %param.15), kind=kLoop, calls=%fused_computation.19 | loop fusion | flops 1048576 | bytes 1572864 | tf_op jit(solution)/shard_map/convert_element_type | solution.py:25
  9.6 0.7 all_to_all.12
  10.2 8.3 %all-to-all-start = ((s32[16,1,32]{2,1,0:T(1,128)}), s32[16,1,32]{2,1,0:T(1,128)S(1)}, u32[]{:S(2)}, u32[]{:S(2)}) async-start(s32[16,1,32]{2,1,0:T(1,128)} %all_to_all.12), calls=%async_computation | async-start | bytes 16384 | tf_op jit(solution)/shard_map/all_to_all | solution.py:29
  18.7 7.1 %all-to-all-done = s32[16,1,32]{2,1,0:T(1,128)S(1)} async-done(((s32[16,1,32]{2,1,0:T(1,128)}), s32[16,1,32]{2,1,0:T(1,128)S(1)}, u32[]{:S(2)}, u32[]{:S(2)}) %all-to-all-start) | async-done | bytes 2080 | tf_op jit(solution)/shard_map/all_to_all | solution.py:29
  25.8 0.5 broadcast.79
  26.3 0.7 reduce.7
  27.0 0.1 reshape.138
  27.1 1.7 %fusion.6 = bf16[1024,256]{1,0:T(8,128)(2,1)S(1)} fusion(bf16[1024,512]{1,0:T(8,128)(2,1)} %all-gather.2.cloned.1.call-done, bf16[256,512]{1,0:T(8,128)(2,1)S(1)} %copy-done.7, f32[1024]{0:T(1024)S(1)} %convert_element_type.29), kind=kOutput, calls=%fused_computation.16 | convolution fusion | flops 268959744 | bytes 1839104 | tf_op jit(solution)/shard_map/dot_general | solution.py:33
  28.8 2.6 %gather_fusion = bf16[512,256]{1,0:T(8,128)(2,1)} fusion(bf16[1024,256]{1,0:T(8,128)(2,1)S(1)} %fusion.6, s32[1024]{0:T(1024)S(1)} %pad_clamp_fusion), kind=kCustom, calls=%fused_computation.1 | custom fusion | bytes 526336 | tf_op jit(solution)/shard_map/gather | solution.py:41
  31.4 3.7 %all-to-all-start.1 = ((bf16[16,32,256]{2,1,0:T(8,128)(2,1)}), bf16[16,32,256]{2,1,0:T(8,128)(2,1)S(1)}, u32[]{:S(2)}, u32[]{:S(2)}) async-start(bf16[16,32,256]{2,1,0:T(8,128)(2,1)} %bitcast.6), calls=%async_computation.1 | async-start | bytes 524288 | tf_op jit(solution)/shard_map/all_to_all | solution.py:42
  35.1 0.0 all-reduce.3.cloned.1.call-start
  35.2 1.3 convolution_bitcast_fusion
  36.4 1.3 convolution_bitcast_fusion.1
  37.7 5.8 %all-to-all-done.1 = bf16[16,32,256]{2,1,0:T(8,128)(2,1)S(1)} async-done(((bf16[16,32,256]{2,1,0:T(8,128)(2,1)}), bf16[16,32,256]{2,1,0:T(8,128)(2,1)S(1)}, u32[]{:S(2)}, u32[]{:S(2)}) %all-to-all-start.1) | async-done | bytes 262176 | tf_op jit(solution)/shard_map/all_to_all | solution.py:42
  43.6 0.1 pad_maximum_fusion
  43.6 0.1 broadcast_in_dim.14
  43.7 78.1 %while.10 = (s32[]{:T(128)}, f32[1536,256]{1,0:T(8,128)S(1)}, s32[2,4096]{1,0:T(2,128)S(1)}, s32[2,4096]{1,0:T(2,128)S(1)}, s32[]{:T(128)}, /*index=5*/s32[2,409...) while((s32[]{:T(128)}, f32[1536,256]{1,0:T(8,128)S(1)}, s32[2,4096]{1,0:T(2,128)S(1)}, ...), condition=%wide.region_2.3_spmd, body=%wide.region_0.2_spmd.sunk | while | flops 3178498 | bytes 2498669 | solution.py:59
  43.8 0.7 compare_reduce_fusion.2
  44.5 38.2 %scatter_custom_fusion.7 = f32[1536,256]{1,0:T(8,128)S(1)} fusion(f32[1536,256]{1,0:T(8,128)S(1)} %get-tuple-element.122, s32[4096]{0:T(1024)S(1)} %bitcast.35, f32[]{:T(128)} %constant.16.clone.1..sunk, pred[4096]{0:T(1024)(128)(4,1)S(1)} %compare_reduce_fusion.2, bf16[1536,256]{1,0:T(8,128)(2,1)S(1)} %get-tuple-element.136, ...), kind=kCustom, calls=%fused_computation.4.clone.1 | custom fusion | flops 3145728 | bytes 2379780 | tf_op jit(solution)/shard_map/while/body/eval_jaxpr/scatter-add | solution.py:57
  82.9 0.7 compare_reduce_fusion.2
  83.6 38.2 %scatter_custom_fusion.7 = f32[1536,256]{1,0:T(8,128)S(1)} fusion(f32[1536,256]{1,0:T(8,128)S(1)} %get-tuple-element.122, s32[4096]{0:T(1024)S(1)} %bitcast.35, f32[]{:T(128)} %constant.16.clone.1..sunk, pred[4096]{0:T(1024)(128)(4,1)S(1)} %compare_reduce_fusion.2, bf16[1536,256]{1,0:T(8,128)(2,1)S(1)} %get-tuple-element.136, ...), kind=kCustom, calls=%fused_computation.4.clone.1 | custom fusion | flops 3145728 | bytes 2379780 | tf_op jit(solution)/shard_map/while/body/eval_jaxpr/scatter-add | solution.py:57
  121.9 0.7 slice.20
  122.6 3.7 %all-to-all-start.2 = ((bf16[16,32,256]{2,1,0:T(8,128)(2,1)}), bf16[16,32,256]{2,1,0:T(8,128)(2,1)S(1)}, u32[]{:S(2)}, u32[]{:S(2)}) async-start(bf16[16,32,256]{2,1,0:T(8,128)(2,1)} %bitcast.8), calls=%async_computation.2 | async-start | bytes 524288 | tf_op jit(solution)/shard_map/all_to_all | solution.py:65
  126.3 0.1 reshape.169
  126.4 1.7 %convolution_add_fusion = f32[1024,256]{1,0:T(8,128)S(1)} fusion(bf16[1024,512]{1,0:T(8,128)(2,1)} %all-gather.2.cloned.1.call-done, bf16[256,512]{1,0:T(8,128)(2,1)} %param.17, f32[1536,256]{1,0:T(8,128)S(1)} %get-tuple-element.40), kind=kOutput, calls=%fused_computation.15 | convolution fusion | flops 268697600 | bytes 3407872 | tf_op jit(solution)/shard_map/dot_general | solution.py:32
  128.1 8.7 %all-to-all-done.2 = bf16[16,32,256]{2,1,0:T(8,128)(2,1)S(1)} async-done(((bf16[16,32,256]{2,1,0:T(8,128)(2,1)}), bf16[16,32,256]{2,1,0:T(8,128)(2,1)S(1)}, u32[]{:S(2)}, u32[]{:S(2)}) %all-to-all-start.2) | async-done | bytes 262176 | tf_op jit(solution)/shard_map/all_to_all | solution.py:65
  136.8 3.7 %scatter_custom_fusion.1 = f32[1024,256]{1,0:T(8,128)S(1)} fusion(f32[1024,256]{1,0:T(8,128)S(1)} %convolution_add_fusion, s32[512]{0:T(512)S(1)} %reshape.169, bf16[512,256]{1,0:T(8,128)(2,1)S(1)} %bitcast.33), kind=kCustom, calls=%fused_computation.22 | custom fusion | flops 262144 | bytes 1310720 | tf_op jit(solution)/shard_map/scatter-add | solution.py:68
  140.6 0.8 convert_element_type.33
  141.4 14.3 %all-reduce.3.cloned.1.call-done = (f32[256,512]{0,1:T(8,128)}, f32[256,512]{0,1:T(8,128)}) async-done(((f32[256,512]{0,1:T(8,128)}, f32[256,512]{0,1:T(8,128)}), (f32[256,512]{0,1:T(8,128)}, f32[256,512]{0,1:T(8,128)})) %all-reduce.3.cloned.1.call-update) | async-done | bytes 1048592 | tf_op jit(solution)/shard_map/psum | solution.py:74
  155.7 2.0 %copy.16 = f32[256,512]{1,0:T(8,128)} copy(f32[256,512]{0,1:T(8,128)} %get-tuple-element.61) | data formatting | bytes 1048576
  157.7 2.0 %copy.17 = f32[256,512]{1,0:T(8,128)} copy(f32[256,512]{0,1:T(8,128)} %get-tuple-element.62) | data formatting | bytes 1048576
  (29 shorter events, 0.3 us)
Async XLA Ops:
  7.2 28.0 %copy-start = (bf16[1024,256]{1,0:T(8,128)(2,1)S(1)}, bf16[1024,256]{1,0:T(8,128)(2,1)}, u32[]{:S(2)}) copy-start(bf16[1024,256]{1,0:T(8,128)(2,1)} %param.16) | copy-start | bytes 1572868
  7.2 2.4 %copy-start.5 = (s32[512]{0:T(512)S(1)}, s32[512]{0:T(512)}, u32[]{:S(2)}) copy-start(s32[512]{0:T(512)} %param.22) | copy-start | bytes 6148
  7.2 11.4 %copy-start.4 = (s32[1024]{0:T(1024)S(1)}, s32[1024]{0:T(1024)}, u32[]{:S(2)}) copy-start(s32[1024]{0:T(1024)} %param.23) | copy-start | bytes 12292
  7.2 11.4 %copy-start.2 = (s32[8192]{0:T(1024)S(1)}, s32[8192]{0:T(1024)}, u32[]{:S(2)}) copy-start(s32[8192]{0:T(1024)} %param.19) | copy-start | bytes 98308
  7.2 11.5 %copy-start.3 = (s32[8192]{0:T(1024)S(1)}, s32[8192]{0:T(1024)}, u32[]{:S(2)}) copy-start(s32[8192]{0:T(1024)} %param.20) | copy-start | bytes 98308
  7.2 19.9 %copy-start.7 = (bf16[256,512]{1,0:T(8,128)(2,1)S(1)}, bf16[256,512]{1,0:T(8,128)(2,1)}, u32[]{:S(2)}) copy-start(bf16[256,512]{1,0:T(8,128)(2,1)} %param.18) | copy-start | bytes 786436
  7.2 19.9 %all-gather.2.cloned.1.call-start = ((), (), s32[]{:S(2)}) async-start(), calls=%async_computation.3 | async-start | bytes 1572864 | tf_op jit(solution)/shard_map/all_gather | solution.py:30
  10.2 15.6 %all-to-all-start = ((s32[16,1,32]{2,1,0:T(1,128)}), s32[16,1,32]{2,1,0:T(1,128)S(1)}, u32[]{:S(2)}, u32[]{:S(2)}) async-start(s32[16,1,32]{2,1,0:T(1,128)} %all_to_all.12), calls=%async_computation | async-start | bytes 16384 | tf_op jit(solution)/shard_map/all_to_all | solution.py:29
  28.8 6.3 %copy-start.1 = (bf16[1024,512]{1,0:T(8,128)(2,1)S(1)}, bf16[1024,512]{1,0:T(8,128)(2,1)}, u32[]{:S(2)}) copy-start(bf16[1024,512]{1,0:T(8,128)(2,1)} %all-gather.2.cloned.1.call-done) | copy-start | bytes 3145732
  31.4 5.0 %copy-start.6 = (bf16[1024,256]{1,0:T(8,128)(2,1)S(1)}, bf16[1024,256]{1,0:T(8,128)(2,1)}, u32[]{:S(2)}) copy-start(bf16[1024,256]{1,0:T(8,128)(2,1)} %param.13) | copy-start | bytes 1572868
  31.4 12.1 %all-to-all-start.1 = ((bf16[16,32,256]{2,1,0:T(8,128)(2,1)}), bf16[16,32,256]{2,1,0:T(8,128)(2,1)S(1)}, u32[]{:S(2)}, u32[]{:S(2)}) async-start(bf16[16,32,256]{2,1,0:T(8,128)(2,1)} %bitcast.6), calls=%async_computation.1 | async-start | bytes 524288 | tf_op jit(solution)/shard_map/all_to_all | solution.py:42
  35.1 120.6 %all-reduce.3.cloned.1.call-start = ((), (), s32[]{:S(2)}) async-start(), calls=%async_computation.4 | async-start | bytes 2097152 | tf_op jit(solution)/shard_map/psum | solution.py:74
  122.6 14.2 %all-to-all-start.2 = ((bf16[16,32,256]{2,1,0:T(8,128)(2,1)}), bf16[16,32,256]{2,1,0:T(8,128)(2,1)S(1)}, u32[]{:S(2)}, u32[]{:S(2)}) async-start(bf16[16,32,256]{2,1,0:T(8,128)(2,1)} %bitcast.8), calls=%async_computation.2 | async-start | bytes 524288 | tf_op jit(solution)/shard_map/all_to_all | solution.py:65
Sparse Core Ops, SparseCore 0:
  10.1 11.4 all-gather.1
  41.8 113.8 all-reduce.2
where the time goes:
time: 167 us
  other arithmetic  85.6 us (51%)
  waiting for transfers between devices  36 us (22%)
  starting transfers between devices  15.8 us (9%)
  between operations  14.3 us (9%)
  local copies, waits for them, and re-layouts  8.92 us (5%)
  matrix products  5.96 us (4%)
    scatter-add x2, other arithmetic, add_block(): return (summed.at[sources].add(contrib), None)  76.5 us
    psum x1, waiting for transfers between devices, on_device(): lax.psum((grad_self, grad_neigh), 'dom')  14.3 us
    all_to_all x1, waiting for transfers between devices, on_device(): lax.all_to_all(mirror_grad.reshape(parts, slots, width_loc), 'dom', split...  8.71 us
    all_to_all x1, starting transfers between devices, on_device(): lax.all_to_all(wanted, 'dom', split_axis=0, concat_axis=0, tiled=True)  8.34 us
    all_to_all x1, waiting for transfers between devices, on_device(): lax.all_to_all(wanted, 'dom', split_axis=0, concat_axis=0, tiled=True)  7.11 us
    all_to_all x1, waiting for transfers between devices, on_device(): lax.all_to_all(replies, 'dom', split_axis=0, concat_axis=0, tiled=True)  5.83 us
    unnamed x18, local copies, waits for them, and re-layouts  4.11 us
    scatter-add x1, other arithmetic, on_device(): jax.ops.segment_sum(returned.reshape(mirror_count, width_loc).astype(jnp....  3.75 us
  transfers between devices with their start and end apart: 5, of which 4 were waited for; matrix products, arithmetic and copies ran while one was open for 54% of the time, Pallas kernels for 0%

commit v1 on v0

--- a/solution.py
+++ b/solution.py
@@ -1,7 +1,71 @@
+import functools
+
 import jax
 import jax.numpy as jnp
 from jax import lax
+from jax.experimental import pallas as pl
+from jax.experimental.pallas import tpu as pltpu
 from jax.sharding import PartitionSpec as P
+
+
+LANES = 128
+HUBS = 64
+
+
+def edge_kernel(block, limit_ref, table_ref, sink_ref, source_ref, out_ref):
+    rows = table_ref.shape[0]
+    groups = block // LANES
+    one, zero = jnp.bfloat16(1.0), jnp.bfloat16(0.0)
+    limit = limit_ref[0]
+    out_ref[...] = jnp.zeros_like(out_ref)
+
+    def step(b, carry):
+        at = pl.ds(pl.multiple_of(b * groups, groups), groups)
+        sinks, sources = sink_ref[at, :], source_ref[at, :]
+        shape = (groups, LANES)
+        place = (
+            lax.broadcasted_iota(jnp.int32, shape, 0) * LANES
+            + lax.broadcasted_iota(jnp.int32, shape, 1)
+            + b * block
+        )
+        sources = jnp.where(place < limit, sources, -1)
+        lane = lax.broadcasted_iota(jnp.int32, (LANES, LANES), 1)
+        pick = []
+        for g in range(groups):
+            column = jnp.transpose(jnp.broadcast_to(sinks[g : g + 1, :], (LANES, LANES)))
+            pick.append(
+                jnp.concatenate(
+                    [
+                        jnp.where(column == lane + j, one, zero)
+                        for j in range(0, rows, LANES)
+                    ],
+                    axis=1,
+                )
+            )
+        pick = jnp.concatenate(pick, axis=0)
+        gathered = jnp.dot(pick, table_ref[...], preferred_element_type=jnp.float32)
+        row = lax.broadcasted_iota(jnp.int32, (rows, LANES), 0)
+        put = jnp.concatenate(
+            [jnp.where(row == sources[g : g + 1, :], one, zero) for g in range(groups)], axis=1
+        )
+        out_ref[...] += jnp.dot(
+            put, gathered.astype(jnp.bfloat16), preferred_element_type=jnp.float32
+        )
+        return carry
+
+    lax.fori_loop(0, sink_ref.shape[0] // groups, step, 0)
+
+
+def edge_sums(limit, table, sinks, sources):
+    edges = sinks.shape[0]
+    vmem = pl.BlockSpec(memory_space=pltpu.VMEM)
+    return pl.pallas_call(
+        functools.partial(edge_kernel, 1024 if table.shape[0] <= 2048 else 256),
+        out_shape=jax.ShapeDtypeStruct(table.shape, jnp.float32),
+        in_specs=[pl.BlockSpec(memory_space=pltpu.SMEM), vmem, vmem, vmem],
+        out_specs=vmem,
+        compiler_params=pltpu.CompilerParams(vmem_limit_bytes=60 * 2**20),
+    )(limit, table, sinks.reshape(-1, LANES), sources.reshape(-1, LANES))
 
 
 def on_device(
@@ -43,34 +107,17 @@
         mirror_count, width_loc
     )
     tables = jnp.concatenate([scaled, mirror_rows], axis=0)
-    local_rows = tables.shape[0]
-    edges = edge_from.shape[0]
-    block_len = min(edges, 4096)
-    blocks = edges // block_len
-    positions = jnp.arange(edges, dtype=jnp.int32).reshape(blocks, block_len)
-    limit = edge_count[0]
-
-    def add_block(summed, pieces):
-        sources, sinks, places = pieces
-        is_live = places < limit
-        contrib = jnp.where(is_live[:, None], tables[sinks].astype(jnp.float32), jnp.float32(0.0))
-        return (summed.at[sources].add(contrib), None)
-
-    summed, unused = lax.scan(
-        add_block,
-        jnp.zeros((local_rows, width_loc), jnp.float32),
-        (edge_from.reshape(blocks, block_len), edge_to.reshape(blocks, block_len), positions),
-    )
+    summed = edge_sums(edge_count, tables, edge_to, edge_from)
     mirror_grad = summed[masters:].astype(jnp.bfloat16)
     returned = lax.all_to_all(
         mirror_grad.reshape(parts, slots, width_loc), "dom", split_axis=0, concat_axis=0, tiled=True
     )
-    master_add = jax.ops.segment_sum(
-        returned.reshape(mirror_count, width_loc).astype(jnp.float32),
-        asked.reshape(-1),
-        num_segments=masters,
+    hit = (jnp.arange(HUBS, dtype=jnp.int32)[:, None] == asked.reshape(1, -1)).astype(jnp.bfloat16)
+    hub_add = jnp.dot(
+        hit, returned.reshape(mirror_count, width_loc), preferred_element_type=jnp.float32
     )
-    input_grad = (self_part + summed[:masters] + master_add).astype(jnp.bfloat16)
+    total = self_part + summed[:masters]
+    input_grad = jnp.concatenate([total[:HUBS] + hub_add, total[HUBS:]], axis=0).astype(jnp.bfloat16)
     self_weight_grad, neigh_weight_grad = lax.psum((grad_self, grad_neigh), "dom")
     return (input_grad, self_weight_grad, neigh_weight_grad)
 

time: 167 us -> 167 us (level)
  other arithmetic: 85.6 us -> 4.68 us
  waiting for transfers between devices: 36 us -> 85.8 us
  Pallas kernels: 0 us -> 29.3 us
    scatter-add x3 -> x0, other arithmetic: 80.2 us -> none  [the longest x2 76.5 us: add_block(): return (summed.at[sources].add(contrib), None)]
    psum x1, waiting for transfers between devices: 14.3 us -> 66.2 us  [on_device(): lax.psum((grad_self, grad_neigh), 'dom')]
    pallas_call x0 -> x1, Pallas kernels: none -> 29.3 us  [edge_sums(): pl.pallas_call(functools.partial(edge_kernel, 1024 if table.shape[0] <= 2...]
    unnamed x18 -> x16, local copies, waits for them, and re-layouts: 4.11 us -> 4.1 us
  transfers between devices with their start and end apart: 5 -> 5, of which waited for: 4 -> 4; matrix products, arithmetic and copies ran while one was open for 54% -> 6% of each run, Pallas kernels for 0% -> 18%
where the time goes in v1:
time: 167 us; the launch traced here: 166 us
  waiting for transfers between devices  85.8 us (51%)
  Pallas kernels  29.3 us (18%)
  starting transfers between devices  15.8 us (9%)
  between operations  14.8 us (9%)
  local copies, waits for them, and re-layouts  9.86 us (6%)
  matrix products  6.1 us (4%)
  other arithmetic  4.68 us (3%)
    psum x1, waiting for transfers between devices, on_device(): lax.psum((grad_self, grad_neigh), 'dom')  66.2 us
    pallas_call x1, Pallas kernels, edge_sums(): pl.pallas_call(functools.partial(edge_kernel, 1024 if table.shape[0] <= 2...  29.3 us
    all_to_all x1, starting transfers between devices, on_device(): lax.all_to_all(wanted, 'dom', split_axis=0, concat_axis=0, tiled=True)  8.34 us
    all_to_all x1, waiting for transfers between devices, on_device(): lax.all_to_all(mirror_grad.reshape(parts, slots, width_loc), 'dom', split...  7.17 us
    all_to_all x1, waiting for transfers between devices, on_device(): lax.all_to_all(wanted, 'dom', split_axis=0, concat_axis=0, tiled=True)  6.55 us
    all_to_all x1, waiting for transfers between devices, on_device(): lax.all_to_all(replies, 'dom', split_axis=0, concat_axis=0, tiled=True)  5.83 us
    unnamed x16, local copies, waits for them, and re-layouts  4.1 us
    all_to_all x1, starting transfers between devices, on_device(): lax.all_to_all(mirror_grad.reshape(parts, slots, width_loc), 'dom', split...  3.7 us
  transfers between devices with their start and end apart: 5, of which 4 were waited for; matrix products, arithmetic and copies ran while one was open for 6% of the time, Pallas kernels for 18%

profile of v1, /device:TPU:0, one launch (start us, length us, event | category | flops | bytes accessed | tf_op | source)
XLA Modules:
  0.0 166.4 jit_solution(11167052814389539355)
XLA Ops:
  7.2 0.0 copy-start
  7.2 0.0 all-gather.2.cloned.1.call-start
  7.3 2.2 %select_convert_fusion = bf16[1024,256]{1,0:T(8,128)(2,1)} fusion(bf16[1024,256]{1,0:T(8,128)(2,1)} %param.12, bf16[1024,256]{1,0:T(8,128)(2,1)} %param.13), kind=kLoop, calls=%fused_computation.8 | loop fusion | flops 1048576 | bytes 1572864 | tf_op jit(solution)/shard_map/convert_element_type | solution.py:89
  9.5 0.0 all-gather.2.cloned.1.call-update
  9.5 0.7 all_to_all.12
  10.2 8.3 %all-to-all-start = ((s32[16,1,32]{2,1,0:T(1,128)}), s32[16,1,32]{2,1,0:T(1,128)S(1)}, u32[]{:S(2)}, u32[]{:S(2)}) async-start(s32[16,1,32]{2,1,0:T(1,128)} %all_to_all.12), calls=%async_computation | async-start | bytes 16384 | tf_op jit(solution)/shard_map/all_to_all | solution.py:93
  19.2 6.6 %all-to-all-done = s32[16,1,32]{2,1,0:T(1,128)S(1)} async-done(((s32[16,1,32]{2,1,0:T(1,128)}), s32[16,1,32]{2,1,0:T(1,128)S(1)}, u32[]{:S(2)}, u32[]{:S(2)}) %all-to-all-start) | async-done | bytes 2080 | tf_op jit(solution)/shard_map/all_to_all | solution.py:93
  25.8 0.5 broadcast.29
  26.3 0.7 reduce.5
  27.0 0.1 reshape.65
  27.1 0.0 all-gather.2.cloned.1.call-done
  27.1 1.7 %fusion = bf16[1024,256]{1,0:T(8,128)(2,1)S(1)} fusion(bf16[1024,512]{1,0:T(8,128)(2,1)} %all-gather.2.cloned.1.call-done, bf16[256,512]{1,0:T(8,128)(2,1)S(1)} %copy-done.6, f32[1024]{0:T(1024)S(1)} %convert_element_type.19), kind=kOutput, calls=%fused_computation.3 | convolution fusion | flops 268959744 | bytes 1839104 | tf_op jit(solution)/shard_map/dot_general | solution.py:97
  28.8 2.6 %gather_fusion = bf16[512,256]{1,0:T(8,128)(2,1)} fusion(bf16[1024,256]{1,0:T(8,128)(2,1)S(1)} %fusion, s32[1024]{0:T(1024)S(1)} %pad_clamp_fusion), kind=kCustom, calls=%fused_computation | custom fusion | bytes 526336 | tf_op jit(solution)/shard_map/gather | solution.py:105
  31.4 3.7 %all-to-all-start.1 = ((bf16[16,32,256]{2,1,0:T(8,128)(2,1)}), bf16[16,32,256]{2,1,0:T(8,128)(2,1)S(1)}, u32[]{:S(2)}, u32[]{:S(2)}) async-start(bf16[16,32,256]{2,1,0:T(8,128)(2,1)} %bitcast.1), calls=%async_computation.1 | async-start | bytes 524288 | tf_op jit(solution)/shard_map/all_to_all | solution.py:106
  35.1 0.0 all-reduce.3.cloned.1.call-start
  35.1 1.3 convolution_bitcast_fusion
  36.4 1.3 convolution_bitcast_fusion.1
  37.7 0.0 all-reduce.3.cloned.1.call-update
  37.7 5.8 %all-to-all-done.1 = bf16[16,32,256]{2,1,0:T(8,128)(2,1)S(1)} async-done(((bf16[16,32,256]{2,1,0:T(8,128)(2,1)}), bf16[16,32,256]{2,1,0:T(8,128)(2,1)S(1)}, u32[]{:S(2)}, u32[]{:S(2)}) %all-to-all-start.1) | async-done | bytes 262176 | tf_op jit(solution)/shard_map/all_to_all | solution.py:106
  43.5 0.9 pad_maximum_fusion.table_ref
  44.5 29.3 %shard_map.130 = f32[1536,256]{1,0:T(8,128)} custom-call(s32[1]{0:T(128)S(6)} %copy.18.limit_ref, bf16[1536,256]{1,0:T(8,128)(2,1)} %pad_maximum_fusion.table_ref, s32[64,128]{1,0:T(8,128)} %bitcast.24, s32[64,128]{1,0:T(8,128)} %bitcast.25), custom_call_target="tpu_custom_call" | custom-call | tf_op jit(solution)/shard_map/pallas_call | solution.py:62
  73.8 1.8 %slice.29 = bf16[512,256]{1,0:T(8,128)(2,1)} slice(f32[1536,256]{1,0:T(8,128)} %shard_map.130), slice={[1024:1536], [0:256]} | slice | bytes 524288 | tf_op jit(solution)/shard_map/slice | solution.py:111
  75.6 3.7 %all-to-all-start.2 = ((bf16[16,32,256]{2,1,0:T(8,128)(2,1)}), bf16[16,32,256]{2,1,0:T(8,128)(2,1)S(1)}, u32[]{:S(2)}, u32[]{:S(2)}) async-start(bf16[16,32,256]{2,1,0:T(8,128)(2,1)} %bitcast.5), calls=%async_computation.2 | async-start | bytes 524288 | tf_op jit(solution)/shard_map/all_to_all | solution.py:112
  79.3 0.1 eq.16
  79.4 1.7 %convolution_add_fusion = f32[1024,256]{1,0:T(8,128)S(1)} fusion(bf16[1024,512]{1,0:T(8,128)(2,1)S(1)} %copy-done.1, bf16[256,512]{1,0:T(8,128)(2,1)S(1)} %copy-done.2, f32[1536,256]{1,0:T(8,128)} %shard_map.130), kind=kOutput, calls=%fused_computation.2 | convolution fusion | flops 268697600 | bytes 3407872 | tf_op jit(solution)/shard_map/dot_general | solution.py:96
  81.1 0.1 slice.28
  81.1 7.2 %all-to-all-done.2 = bf16[16,32,256]{2,1,0:T(8,128)(2,1)S(1)} async-done(((bf16[16,32,256]{2,1,0:T(8,128)(2,1)}), bf16[16,32,256]{2,1,0:T(8,128)(2,1)S(1)}, u32[]{:S(2)}, u32[]{:S(2)}) %all-to-all-start.2) | async-done | bytes 262176 | tf_op jit(solution)/shard_map/all_to_all | solution.py:112
  88.3 0.2 fusion.1
  88.5 0.8 pad_maximum_fusion.1
  89.3 66.2 %all-reduce.3.cloned.1.call-done = (f32[256,512]{0,1:T(8,128)}, f32[256,512]{0,1:T(8,128)}) async-done(((f32[256,512]{0,1:T(8,128)}, f32[256,512]{0,1:T(8,128)}), (f32[256,512]{0,1:T(8,128)}, f32[256,512]{0,1:T(8,128)})) %all-reduce.3.cloned.1.call-update) | async-done | bytes 1048592 | tf_op jit(solution)/shard_map/psum | solution.py:121
  155.5 2.0 %copy.14 = f32[256,512]{1,0:T(8,128)} copy(f32[256,512]{0,1:T(8,128)} %get-tuple-element.6) | data formatting | bytes 1048576
  157.6 2.0 %copy.15 = f32[256,512]{1,0:T(8,128)} copy(f32[256,512]{0,1:T(8,128)} %get-tuple-element.7) | data formatting | bytes 1048576
  (16 shorter events, 0.0 us)
Async XLA Ops:
  7.2 27.9 %copy-start = (bf16[1024,256]{1,0:T(8,128)(2,1)S(1)}, bf16[1024,256]{1,0:T(8,128)(2,1)}, u32[]{:S(2)}) copy-start(bf16[1024,256]{1,0:T(8,128)(2,1)} %param.14) | copy-start | bytes 1572868
  7.2 2.3 %copy-start.4 = (s32[512]{0:T(512)S(1)}, s32[512]{0:T(512)}, u32[]{:S(2)}) copy-start(s32[512]{0:T(512)} %param.20) | copy-start | bytes 6148
  7.2 11.4 %copy-start.3 = (s32[1024]{0:T(1024)S(1)}, s32[1024]{0:T(1024)}, u32[]{:S(2)}) copy-start(s32[1024]{0:T(1024)} %param.21) | copy-start | bytes 12292
  7.2 19.9 %copy-start.6 = (bf16[256,512]{1,0:T(8,128)(2,1)S(1)}, bf16[256,512]{1,0:T(8,128)(2,1)}, u32[]{:S(2)}) copy-start(bf16[256,512]{1,0:T(8,128)(2,1)} %param.16) | copy-start | bytes 786436
  7.2 19.9 %all-gather.2.cloned.1.call-start = ((), (), s32[]{:S(2)}) async-start(), calls=%async_computation.3 | async-start | bytes 1572864 | tf_op jit(solution)/shard_map/all_gather | solution.py:94
  10.2 15.6 %all-to-all-start = ((s32[16,1,32]{2,1,0:T(1,128)}), s32[16,1,32]{2,1,0:T(1,128)S(1)}, u32[]{:S(2)}, u32[]{:S(2)}) async-start(s32[16,1,32]{2,1,0:T(1,128)} %all_to_all.12), calls=%async_computation | async-start | bytes 16384 | tf_op jit(solution)/shard_map/all_to_all | solution.py:93
  28.8 6.3 %copy-start.1 = (bf16[1024,512]{1,0:T(8,128)(2,1)S(1)}, bf16[1024,512]{1,0:T(8,128)(2,1)}, u32[]{:S(2)}) copy-start(bf16[1024,512]{1,0:T(8,128)(2,1)} %all-gather.2.cloned.1.call-done) | copy-start | bytes 3145732
  31.4 5.0 %copy-start.5 = (bf16[1024,256]{1,0:T(8,128)(2,1)S(1)}, bf16[1024,256]{1,0:T(8,128)(2,1)}, u32[]{:S(2)}) copy-start(bf16[1024,256]{1,0:T(8,128)(2,1)} %param.11) | copy-start | bytes 1572868
  31.4 12.1 %all-to-all-start.1 = ((bf16[16,32,256]{2,1,0:T(8,128)(2,1)}), bf16[16,32,256]{2,1,0:T(8,128)(2,1)S(1)}, u32[]{:S(2)}, u32[]{:S(2)}) async-start(bf16[16,32,256]{2,1,0:T(8,128)(2,1)} %bitcast.1), calls=%async_computation.1 | async-start | bytes 524288 | tf_op jit(solution)/shard_map/all_to_all | solution.py:106
  35.1 120.5 %all-reduce.3.cloned.1.call-start = ((), (), s32[]{:S(2)}) async-start(), calls=%async_computation.4 | async-start | bytes 2097152 | tf_op jit(solution)/shard_map/psum | solution.py:121
  44.5 34.9 %copy-start.2 = (bf16[256,512]{1,0:T(8,128)(2,1)S(1)}, bf16[256,512]{1,0:T(8,128)(2,1)}, u32[]{:S(2)}) copy-start(bf16[256,512]{1,0:T(8,128)(2,1)} %param.15) | copy-start | bytes 786436
  75.6 12.7 %all-to-all-start.2 = ((bf16[16,32,256]{2,1,0:T(8,128)(2,1)}), bf16[16,32,256]{2,1,0:T(8,128)(2,1)S(1)}, u32[]{:S(2)}, u32[]{:S(2)}) async-start(bf16[16,32,256]{2,1,0:T(8,128)(2,1)} %bitcast.5), calls=%async_computation.2 | async-start | bytes 524288 | tf_op jit(solution)/shard_map/all_to_all | solution.py:112
Sparse Core Ops, SparseCore 0:
  10.1 11.4 all-gather.1
  41.8 113.6 all-reduce.2

commit v2 on v0

v2 whole, which is shorter than its diff:
```python
import functools

import jax
import jax.numpy as jnp
from jax import lax
from jax.experimental import pallas as pl
from jax.experimental.pallas import tpu as pltpu
from jax.sharding import PartitionSpec as P

LANES = 128
HUBS = 64
MESH = pl.DeviceIdType.MESH
F32, BF16 = jnp.float32, jnp.bfloat16


def dot(a, b, over):
    return lax.dot_general(a, b, ((over[:1], over[1:]), ((), ())), preferred_element_type=F32)


def columns_of(row):
    return jnp.transpose(jnp.broadcast_to(row, (LANES, LANES)))


def pick_rows(sinks, first, count):
    one, zero = jnp.ones((), BF16), jnp.zeros((), BF16)
    lane = lax.broadcasted_iota(jnp.int32, (LANES, LANES), 1)
    tiles = []
    for g in range(sinks.shape[0]):
        column = columns_of(sinks[g : g + 1, :])
        tiles.append(
            jnp.concatenate(
                [jnp.where(column == lane + (first + j), one, zero) for j in range(0, count, LANES)],
                axis=1,
            )
        )
    return jnp.concatenate(tiles, axis=0)


def put_rows(sources, first, count):
    one, zero = jnp.ones((), BF16), jnp.zeros((), BF16)
    row = lax.broadcasted_iota(jnp.int32, (count, LANES), 0) + first
    return jnp.concatenate(
        [jnp.where(row == sources[g : g + 1, :], one, zero) for g in range(sources.shape[0])],
        axis=1,
    )


def layer_kernel(
    parts,
    block,
    limit_ref,
    grad_ref,
    pre_ref,
    features_ref,
    mean_ref,
    w_self_ref,
    w_neigh_ref,
    source_ref,
    sink_ref,
    wanted_ref,
    degree_ref,
    out_ref,
    weights_ref,
    cols,
    live,
    table,
    asked,
    replies,
    mirrors,
    picked,
    master_sum,
    mirror_sum,
    returns,
    returned,
    partial,
    arrived,
    summed,
    feat_sems,
    send_sems,
    recv_sems,
):
    me, half = lax.axis_index("dom"), lax.axis_index("feat")
    partner = 1 - half
    masters, width = grad_ref.shape
    slots = wanted_ref.shape[2]
    chunks, chunk = partial.shape[0], partial.shape[1]
    groups = block // LANES
    blocks = sink_ref.shape[0] // groups

    def peer(k):
        return lax.rem(me + k, parts)

    def giver(k):
        return lax.rem(me + (parts - k), parts)

    def rows_of(q):
        return pl.ds(pl.multiple_of(q * slots, slots), slots)

    def copy(stage, k, src, dst):
        return pltpu.make_async_remote_copy(
            src_ref=src,
            dst_ref=dst,
            send_sem=send_sems.at[stage, k],
            recv_sem=recv_sems.at[stage, k],
            device_id={"dom": peer(k)},
            device_id_type=MESH,
        )

    def each_peer(act):
        lax.fori_loop(1, parts, lambda k, c: (act(k), c)[1], 0)

    barrier = pltpu.get_barrier_semaphore()
    pl.semaphore_signal(barrier, inc=1, device_id={"feat": partner}, device_id_type=MESH)
    each_peer(
        lambda k: pl.semaphore_signal(
            barrier, inc=1, device_id={"dom": peer(k)}, device_id_type=MESH
        )
    )
    keep = (pre_ref[...] > 0).astype(F32)
    cols[half] = (grad_ref[...].astype(F32) * keep).astype(BF16)
    place = (
        lax.broadcasted_iota(jnp.int32, source_ref.shape, 0) * LANES
        + lax.broadcasted_iota(jnp.int32, source_ref.shape, 1)
    )
    live[...] = jnp.where(place < limit_ref[0], source_ref[...], -1)
    asked[me] = wanted_ref[me]
    pl.semaphore_wait(barrier, parts)

    exchange = pltpu.make_async_remote_copy(
        src_ref=cols.at[half],
        dst_ref=cols.at[half],
        send_sem=feat_sems.at[0],
        recv_sem=feat_sems.at[1],
        device_id={"feat": partner},
        device_id_type=MESH,
    )
    exchange.start()

    def request(k):
        return copy(0, k, wanted_ref.at[peer(k)], asked.at[me])

    each_peer(lambda k: request(k).start())
    pltpu.make_async_remote_copy(
        src_ref=cols.at[half],
        dst_ref=cols.at[partner],
        send_sem=feat_sems.at[0],
        recv_sem=feat_sems.at[1],
        device_id={"feat": partner},
        device_id_type=MESH,
    ).wait_recv()

    neigh = dot(cols[0], w_neigh_ref[:, :width], (1, 1)) + dot(
        cols[1], w_neigh_ref[:, width:], (1, 1)
    )
    for g in range(masters // LANES):
        at = slice(g * LANES, (g + 1) * LANES)
        degree = columns_of(degree_ref[g : g + 1, :]).astype(F32)
        degree = jnp.concatenate([degree] * (width // LANES), axis=1)
        table[at, :] = (neigh[at, :] / degree).astype(BF16)

    each_peer(lambda k: copy(0, k, wanted_ref.at[peer(k)], asked.at[giver(k)]).wait_recv())

    def hits(q):
        hub = lax.broadcasted_iota(jnp.int32, (HUBS, slots), 0)
        return jnp.where(hub == asked[q], jnp.ones((), BF16), jnp.zeros((), BF16))

    def answer(k, c):
        q = peer(k)
        replies[rows_of(q), :] = dot(hits(q), table[:HUBS, :], (0, 0)).astype(BF16)
        return c

    lax.fori_loop(0, parts, answer, 0)
    mirrors[rows_of(me), :] = replies[rows_of(me), :]

    def reply(k):
        return copy(1, k, replies.at[rows_of(peer(k)), :], mirrors.at[rows_of(me), :])

    each_peer(lambda k: reply(k).start())

    per_weight = chunks // 2
    for i, operand in enumerate((features_ref, mean_ref)):
        for h in range(2):
            part = dot(operand[...], cols[h], (0, 0)).astype(BF16)
            for c in range(per_weight):
                partial[i * per_weight + c, :, h * width : (h + 1) * width] = part[
                    c * chunk : (c + 1) * chunk, :
                ]

    def guarded(act, owner):
        if chunks == parts:
            return act
        return lambda k: pl.when(owner(k) < chunks)(lambda: act(k))

    def scatter(k):
        return copy(2, k, partial.at[lax.rem(peer(k), chunks)], arrived.at[me])

    each_peer(guarded(lambda k: scatter(k).start(), peer))
    master_sum[...] = dot(cols[0], w_self_ref[:, :width], (1, 1)) + dot(
        cols[1], w_self_ref[:, width:], (1, 1)
    )

    def block_at(b):
        return pl.ds(pl.multiple_of(b * groups, groups), groups)

    def edges_at(b):
        return pl.ds(pl.multiple_of(b * block, block), block)

    def from_masters(b, c):
        pick = pick_rows(sink_ref[block_at(b), :], 0, masters)
        picked[edges_at(b), :] = dot(pick, table[...], (1, 0)).astype(BF16)
        return c

    lax.fori_loop(0, blocks, from_masters, 0)

    each_peer(
        lambda k: copy(
            1, k, replies.at[rows_of(peer(k)), :], mirrors.at[rows_of(giver(k)), :]
        ).wait_recv()
    )
    mirror_sum[...] = jnp.zeros_like(mirror_sum)
    mirror_count = mirrors.shape[0]

    def from_mirrors(b, c):
        pick = pick_rows(sink_ref[block_at(b), :], masters, mirror_count)
        more = dot(pick, mirrors[...], (1, 0)).astype(BF16)
        row = picked[edges_at(b), :] + more
        picked[edges_at(b), :] = row
        put = put_rows(live[block_at(b), :], masters, mirror_count)
        mirror_sum[...] += dot(put, row, (1, 0))
        return c

    lax.fori_loop(0, blocks, from_mirrors, 0)
    returns[...] = mirror_sum[...].astype(BF16)
    returned[rows_of(me), :] = returns[rows_of(me), :]

    def give_back(k):
        return copy(3, k, returns.at[rows_of(peer(k)), :], returned.at[rows_of(me), :])

    each_peer(lambda k: give_back(k).start())

    def reduce_chunk():
        arrived[me] = partial[lax.rem(me, chunks)]
        each_peer(
            lambda k: copy(
                2, k, partial.at[lax.rem(peer(k), chunks)], arrived.at[giver(k)]
            ).wait_recv()
        )
        total = lax.fori_loop(
            0,
            parts,
            lambda p, t: t + arrived[p].astype(F32),
            jnp.zeros(partial.shape[1:], F32),
        )
        summed[lax.rem(me, chunks)] = total.astype(BF16)

    def spread(k):
        return copy(4, k, summed.at[lax.rem(me, chunks)], summed.at[lax.rem(me, chunks)])

    def reduce_and_spread():
        reduce_chunk()
        each_peer(lambda k: spread(k).start())

    if chunks == parts:
        reduce_and_spread()
    else:
        pl.when(me < chunks)(reduce_and_spread)

    def to_masters(b, c):
        put = put_rows(live[block_at(b), :], 0, masters)
        master_sum[...] += dot(put, picked[edges_at(b), :], (1, 0))
        return c

    lax.fori_loop(0, blocks, to_masters, 0)

    each_peer(
        lambda k: copy(
            3, k, returns.at[rows_of(peer(k)), :], returned.at[rows_of(giver(k)), :]
        ).wait_recv()
    )
    hub_sum = lax.fori_loop(
        0,
        parts,
        lambda q, t: t + dot(hits(q), returned[rows_of(q), :], (1, 0)),
        master_sum[:HUBS, :],
    )
    out_ref[:HUBS, :] = hub_sum.astype(BF16)
    out_ref[HUBS:, :] = master_sum[HUBS:, :].astype(BF16)

    each_peer(
        guarded(
            lambda k: copy(
                4,
                k,
                summed.at[lax.rem(me, chunks)],
                summed.at[lax.rem(giver(k), chunks)],
            ).wait_recv(),
            giver,
        )
    )
    weights_ref[...] = summed[...]

    exchange.wait_send()
    each_peer(lambda k: request(k).wait_send())
    each_peer(lambda k: reply(k).wait_send())
    each_peer(guarded(lambda k: scatter(k).wait_send(), peer))
    each_peer(lambda k: give_back(k).wait_send())
    each_peer(guarded(lambda k: spread(k).wait_send(), lambda k: me))


def on_device(
    features,
    grad_out,
    pre_act,
    neigh_mean,
    w_self,
    w_neigh,
    edge_from,
    edge_to,
    edge_count,
    mirror_master,
    degrees,
):
    masters, width = features.shape
    parts = lax.axis_size("dom")
    mirror_count = mirror_master.shape[0]
    slots = mirror_count // parts
    edges = edge_from.shape[0]
    full = w_self.shape[1]
    weight_rows = 2 * w_self.shape[0]
    chunks = min(parts, weight_rows // 16)
    chunk = weight_rows // chunks
    block = min(edges, 1024 if masters + mirror_count <= 2048 else 256)
    vmem = pl.BlockSpec(memory_space=pltpu.VMEM)
    input_grad, weights = pl.pallas_call(
        functools.partial(layer_kernel, parts, block),
        out_shape=(
            jax.ShapeDtypeStruct((masters, width), BF16),
            jax.ShapeDtypeStruct((chunks, chunk, full), BF16),
        ),
        in_specs=[pl.BlockSpec(memory_space=pltpu.SMEM)] + [vmem] * 10,
        out_specs=(vmem, vmem),
        scratch_shapes=[
            pltpu.VMEM((2, masters, width), BF16),
            pltpu.VMEM((edges // LANES, LANES), jnp.int32),
            pltpu.VMEM((masters, width), BF16),
            pltpu.VMEM((parts, 1, slots), jnp.int32),
            pltpu.VMEM((mirror_count, width), BF16),
            pltpu.VMEM((mirror_count, width), BF16),
            pltpu.VMEM((edges, width), BF16),
            pltpu.VMEM((masters, width), F32),
            pltpu.VMEM((mirror_count, width), F32),
            pltpu.VMEM((mirror_count, width), BF16),
            pltpu.VMEM((mirror_count, width), BF16),
            pltpu.VMEM((chunks, chunk, full), BF16),
            pltpu.VMEM((parts, chunk, full), BF16),
            pltpu.VMEM((chunks, chunk, full), BF16),
            pltpu.SemaphoreType.DMA((2,)),
            pltpu.SemaphoreType.DMA((5, parts)),
            pltpu.SemaphoreType.DMA((5, parts)),
        ],
        compiler_params=pltpu.CompilerParams(
            collective_id=0, has_side_effects=True, vmem_limit_bytes=60 * 2**20
        ),
    )(
        edge_count,
        grad_out,
        pre_act,
        features,
        neigh_mean,
        w_self,
        w_neigh,
        edge_from.reshape(-1, LANES),
        edge_to.reshape(-1, LANES),
        mirror_master.reshape(parts, 1, slots),
        degrees.reshape(-1, LANES),
    )
    weights = weights.reshape(2, w_self.shape[0], full).astype(F32)
    return (input_grad, weights[0], weights[1])


def solution(mesh):
    placed = (
        P("dom", "feat"),
        P("dom", "feat"),
        P("dom", "feat"),
        P("dom", "feat"),
        P("feat", None),
        P("feat", None),
        P("dom"),
        P("dom"),
        P("dom"),
        P("dom"),
        P("dom"),
    )
    return jax.shard_map(
        on_device,
        mesh=mesh,
        in_specs=placed,
        out_specs=(P("dom", "feat"), P("feat", None), P("feat", None)),
        check_vma=False,
    )
```

time: 167 us -> 56.9 us (0.34)
  other arithmetic: 85.6 us -> 0 us
  Pallas kernels: 0 us -> 50.8 us
  waiting for transfers between devices: 36 us -> 0 us
  starting transfers between devices: 15.8 us -> 0 us
  between operations: 14.3 us -> 1.3 us
  matrix products: 5.96 us -> 0 us
  local copies, waits for them, and re-layouts: 8.92 us -> 4.34 us
    scatter-add x3 -> x0, other arithmetic: 80.2 us -> none  [the longest x2 76.5 us: add_block(): return (summed.at[sources].add(contrib), None)]
    pallas_call x0 -> x1, Pallas kernels: none -> 50.8 us  [on_device(): pl.pallas_call(functools.partial(layer_kernel, parts, block), out_shape=(...]
    all_to_all x3 -> x0, waiting for transfers between devices: 21.7 us -> none  [the longest x1 8.71 us: on_device(): lax.all_to_all(mirror_grad.reshape(parts, slots, width_loc), 'dom', split...]
    all_to_all x3 -> x0, starting transfers between devices: 15.7 us -> none  [the longest x1 8.34 us: on_device(): lax.all_to_all(wanted, 'dom', split_axis=0, concat_axis=0, tiled=True)]
    psum x1 -> x0, waiting for transfers between devices: 14.3 us -> none  [on_device(): lax.psum((grad_self, grad_neigh), 'dom')]
    dot_general x4 -> x0, matrix products: 5.96 us -> none  [the longest x1 1.73 us: on_device(): lax.dot_general(block_cols, w_self, contract, preferred_element_type=jnp....]
    convert_element_type x3 -> x0, other arithmetic: 3.09 us -> none  [the longest x1 2.24 us: on_device(): (grad_out.astype(jnp.float32) * (pre_act > 0).astype(jnp.float32)).astype...]
    unnamed x18 -> x5, local copies, waits for them, and re-layouts: 4.11 us -> 1.47 us
  transfers between devices with their start and end apart: 5 -> 0, of which waited for: 4 -> 0; matrix products, arithmetic and copies ran while one was open for 54% -> 0% of each run, Pallas kernels for 0% -> 0%
where the time goes in v2:
time: 56.9 us; the launch traced here: 56.4 us
  Pallas kernels  50.8 us (89%)
  local copies, waits for them, and re-layouts  4.34 us (8%)
  between operations  1.3 us (2%)
    pallas_call x1, Pallas kernels, on_device(): pl.pallas_call(functools.partial(layer_kernel, parts, block), out_shape=(...  50.8 us
    slice x1, local copies, waits for them, and re-layouts, on_device(): return (input_grad, weights[0], weights[1])  2.19 us
    unnamed x5, local copies, waits for them, and re-layouts  1.47 us

profile of v2, /device:TPU:0, one launch (start us, length us, event | category | flops | bytes accessed | tf_op | source)
XLA Modules:
  0.0 56.4 jit_solution(12792006047189295158)
XLA Ops:
  1.3 0.0 copy-start.1
  1.3 0.7 %copy-done.1 = s32[512]{0:T(512)S(1)} copy-done((s32[512]{0:T(512)S(1)}, s32[512]{0:T(512)}, u32[]{:S(2)}) %copy-start.1) | copy-done | bytes 2072
  2.0 0.7 %reshape.26.wanted_ref = s32[16,1,32]{2,1,0:T(1,128)} reshape(s32[512]{0:T(512)S(1)} %copy-done.1) | data formatting | bytes 4096 | tf_op jit(solution)/shard_map/reshape | solution.py:374
  2.6 50.8 %shard_map.130 = (bf16[1024,256]{1,0:T(8,128)(2,1)}, bf16[16,32,512]{2,1,0:T(8,128)(2,1)}) custom-call(s32[1]{0:T(128)S(6)} %copy.15.limit_ref, bf16[1024,256]{1,0:T(8,128)(2,1)} %grad_ref.1, bf16[1024,256]{1,0:T(8,128)(2,1)} %pre_ref.1, bf16[1024,256]{1,0:T(8,128)(2,1)} %features_ref.1, bf16[1024,256]{1,0:T(8,128)(2,1)} %mean_ref.1, ...), custom_call_target="tpu_custom_call" | custom-call | tf_op jit(solution)/shard_map/pallas_call | solution.py:334
  53.4 0.0 copy-start
  53.4 2.2 %fusion = (f32[8,32,512]{2,1,0:T(8,128)}, f32[8,32,512]{2,1,0:T(8,128)}) fusion(bf16[16,32,512]{2,1,0:T(8,128)(2,1)} %get-tuple-element.6), kind=kLoop, calls=%fused_computation | loop fusion | bytes 2097152 | tf_op jit(solution)/shard_map/slice | solution.py:378
  55.6 0.0 copy-done
  55.6 0.8 %copy.16 = bf16[1024,256]{1,0:T(8,128)(2,1)} copy(bf16[1024,256]{1,0:T(8,128)(2,1)S(1)} %copy-done) | data formatting | bytes 1048576
Async XLA Ops:
  1.3 0.7 %copy-start.1 = (s32[512]{0:T(512)S(1)}, s32[512]{0:T(512)}, u32[]{:S(2)}) copy-start(s32[512]{0:T(512)} %param.20) | copy-start | bytes 6148
  53.4 2.2 %copy-start = (bf16[1024,256]{1,0:T(8,128)(2,1)S(1)}, bf16[1024,256]{1,0:T(8,128)(2,1)}, u32[]{:S(2)}) copy-start(bf16[1024,256]{1,0:T(8,128)(2,1)} %get-tuple-element.12) | copy-start | bytes 1572868

commit v3 on v2

--- a/solution.py
+++ b/solution.py
@@ -51,16 +51,20 @@
     limit_ref,
     grad_ref,
     pre_ref,
-    features_ref,
-    mean_ref,
-    w_self_ref,
-    w_neigh_ref,
+    features_hbm,
+    mean_hbm,
+    w_self_hbm,
+    w_neigh_hbm,
     source_ref,
     sink_ref,
     wanted_ref,
     degree_ref,
     out_ref,
     weights_ref,
+    features_ref,
+    mean_ref,
+    w_self_ref,
+    w_neigh_ref,
     cols,
     live,
     table,
@@ -72,9 +76,14 @@
     mirror_sum,
     returns,
     returned,
+    hits,
     partial,
     arrived,
-    summed,
+    column_sum,
+    column_arrived,
+    column_total,
+    full,
+    load_sems,
     feat_sems,
     send_sems,
     recv_sems,
@@ -83,7 +92,10 @@
     partner = 1 - half
     masters, width = grad_ref.shape
     slots = wanted_ref.shape[2]
-    chunks, chunk = partial.shape[0], partial.shape[1]
+    low, low_rows = partial.shape[0], partial.shape[1]
+    owners, chunk = column_sum.shape[0], column_sum.shape[1]
+    high = parts // low
+    at_high, at_low = me // low, lax.rem(me, low)
     groups = block // LANES
     blocks = sink_ref.shape[0] // groups
 
@@ -96,18 +108,30 @@
     def rows_of(q):
         return pl.ds(pl.multiple_of(q * slots, slots), slots)
 
-    def copy(stage, k, src, dst):
+    def copy(stage, k, src, dst, device=None):
         return pltpu.make_async_remote_copy(
             src_ref=src,
             dst_ref=dst,
             send_sem=send_sems.at[stage, k],
             recv_sem=recv_sems.at[stage, k],
-            device_id={"dom": peer(k)},
+            device_id={"dom": peer(k) if device is None else device},
             device_id_type=MESH,
         )
 
-    def each_peer(act):
-        lax.fori_loop(1, parts, lambda k, c: (act(k), c)[1], 0)
+    def each_peer(act, count=parts):
+        lax.fori_loop(1, count, lambda k, c: (act(k), c)[1], 0)
+
+    loads = [
+        pltpu.make_async_copy(src, dst, load_sems.at[i])
+        for i, (src, dst) in enumerate(
+            (
+                (w_neigh_hbm, w_neigh_ref),
+                (features_hbm, features_ref),
+                (mean_hbm, mean_ref),
+                (w_self_hbm, w_self_ref),
+            )
+        )
+    ]
 
     barrier = pltpu.get_barrier_semaphore()
     pl.semaphore_signal(barrier, inc=1, device_id={"feat": partner}, device_id_type=MESH)
@@ -116,6 +140,8 @@
             barrier, inc=1, device_id={"dom": peer(k)}, device_id_type=MESH
         )
     )
+    for load in loads:
+        load.start()
     keep = (pre_ref[...] > 0).astype(F32)
     cols[half] = (grad_ref[...].astype(F32) * keep).astype(BF16)
     place = (
@@ -149,6 +175,7 @@
         device_id_type=MESH,
     ).wait_recv()
 
+    loads[0].wait()
     neigh = dot(cols[0], w_neigh_ref[:, :width], (1, 1)) + dot(
         cols[1], w_neigh_ref[:, width:], (1, 1)
     )
@@ -160,16 +187,25 @@
 
     each_peer(lambda k: copy(0, k, wanted_ref.at[peer(k)], asked.at[giver(k)]).wait_recv())
 
-    def hits(q):
-        hub = lax.broadcasted_iota(jnp.int32, (HUBS, slots), 0)
-        return jnp.where(hub == asked[q], jnp.ones((), BF16), jnp.zeros((), BF16))
-
-    def answer(k, c):
-        q = peer(k)
-        replies[rows_of(q), :] = dot(hits(q), table[:HUBS, :], (0, 0)).astype(BF16)
+    batch = 8 if parts % 8 == 0 else 1
+    hub = lax.broadcasted_iota(jnp.int32, (HUBS, slots), 0)
+
+    def batch_at(i):
+        return pl.ds(pl.multiple_of(i * batch * slots, batch * slots), batch * slots)
+
+    def answer(i, c):
+        hit = jnp.concatenate(
+            [
+                jnp.where(hub == asked[i * batch + j], jnp.ones((), BF16), jnp.zeros((), BF16))
+                for j in range(batch)
+            ],
+            axis=1,
+        )
+        hits[i] = hit
+        replies[batch_at(i), :] = dot(hit, table[:HUBS, :], (0, 0)).astype(BF16)
         return c
 
-    lax.fori_loop(0, parts, answer, 0)
+    lax.fori_loop(0, parts // batch, answer, 0)
     mirrors[rows_of(me), :] = replies[rows_of(me), :]
 
     def reply(k):
@@ -177,24 +213,48 @@
 
     each_peer(lambda k: reply(k).start())
 
-    per_weight = chunks // 2
+    both = jnp.concatenate([cols[0], cols[1]], axis=1)
+    per_weight = low // 2
     for i, operand in enumerate((features_ref, mean_ref)):
-        for h in range(2):
-            part = dot(operand[...], cols[h], (0, 0)).astype(BF16)
-            for c in range(per_weight):
-                partial[i * per_weight + c, :, h * width : (h + 1) * width] = part[
-                    c * chunk : (c + 1) * chunk, :
-                ]
+        loads[1 + i].wait()
+        part = dot(operand[...], both, (0, 0)).astype(BF16)
+        for c in range(per_weight):
+            partial[i * per_weight + c] = part[c * low_rows : (c + 1) * low_rows, :]
+
+    def low_peer(k):
+        return lax.rem(at_low + k, low)
+
+    def low_giver(k):
+        return lax.rem(at_low + (low - k), low)
+
+    def high_peer(k):
+        return lax.rem(at_high + k, high)
+
+    def high_giver(k):
+        return lax.rem(at_high + (high - k), high)
+
+    def to_low(stage, k, src, dst):
+        return copy(stage, k, src, dst, at_high * low + low_peer(k))
+
+    def to_high(stage, k, src, dst):
+        return copy(stage, k, src, dst, high_peer(k) * low + at_low)
 
     def guarded(act, owner):
-        if chunks == parts:
+        if owners == high:
             return act
-        return lambda k: pl.when(owner(k) < chunks)(lambda: act(k))
+        return lambda k: pl.when(owner(k) < owners)(lambda: act(k))
+
+    def if_owner(act):
+        if owners == high:
+            act()
+        else:
+            pl.when(at_high < owners)(act)
 
     def scatter(k):
-        return copy(2, k, partial.at[lax.rem(peer(k), chunks)], arrived.at[me])
-
-    each_peer(guarded(lambda k: scatter(k).start(), peer))
+        return to_low(2, k, partial.at[low_peer(k)], arrived.at[at_low])
+
+    each_peer(lambda k: scatter(k).start(), low)
+    loads[3].wait()
     master_sum[...] = dot(cols[0], w_self_ref[:, :width], (1, 1)) + dot(
         cols[1], w_self_ref[:, width:], (1, 1)
     )
@@ -211,6 +271,28 @@
         return c
 
     lax.fori_loop(0, blocks, from_masters, 0)
+
+    each_peer(
+        lambda k: to_low(2, k, partial.at[low_peer(k)], arrived.at[low_giver(k)]).wait_recv(), low
+    )
+    total = lax.fori_loop(
+        1,
+        low,
+        lambda k, t: t + arrived[low_giver(k)].astype(F32),
+        partial[at_low].astype(F32),
+    ).astype(BF16)
+    for c in range(owners):
+        column_sum[c] = total[c * chunk : (c + 1) * chunk, :]
+
+    def column_place():
+        return lax.rem(at_high, owners)
+
+    def scatter_high(k):
+        return to_high(
+            4, k, column_sum.at[lax.rem(high_peer(k), owners)], column_arrived.at[at_high]
+        )
+
+    each_peer(guarded(lambda k: scatter_high(k).start(), high_peer), high)
 
     each_peer(
         lambda k: copy(
@@ -225,11 +307,16 @@
         more = dot(pick, mirrors[...], (1, 0)).astype(BF16)
         row = picked[edges_at(b), :] + more
         picked[edges_at(b), :] = row
+        return c
+
+    lax.fori_loop(0, blocks, from_mirrors, 0)
+
+    def to_mirrors(b, c):
         put = put_rows(live[block_at(b), :], masters, mirror_count)
-        mirror_sum[...] += dot(put, row, (1, 0))
+        mirror_sum[...] += dot(put, picked[edges_at(b), :], (1, 0))
         return c
 
-    lax.fori_loop(0, blocks, from_mirrors, 0)
+    lax.fori_loop(0, blocks, to_mirrors, 0)
     returns[...] = mirror_sum[...].astype(BF16)
     returned[rows_of(me), :] = returns[rows_of(me), :]
 
@@ -238,39 +325,56 @@
 
     each_peer(lambda k: give_back(k).start())
 
-    def reduce_chunk():
-        arrived[me] = partial[lax.rem(me, chunks)]
+    def column_spread(k):
+        return to_high(5, k, column_total.at[column_place()], column_total.at[column_place()])
+
+    def reduce_column():
         each_peer(
-            lambda k: copy(
-                2, k, partial.at[lax.rem(peer(k), chunks)], arrived.at[giver(k)]
-            ).wait_recv()
-        )
-        total = lax.fori_loop(
-            0,
-            parts,
-            lambda p, t: t + arrived[p].astype(F32),
-            jnp.zeros(partial.shape[1:], F32),
-        )
-        summed[lax.rem(me, chunks)] = total.astype(BF16)
-
-    def spread(k):
-        return copy(4, k, summed.at[lax.rem(me, chunks)], summed.at[lax.rem(me, chunks)])
-
-    def reduce_and_spread():
-        reduce_chunk()
-        each_peer(lambda k: spread(k).start())
-
-    if chunks == parts:
-        reduce_and_spread()
-    else:
-        pl.when(me < chunks)(reduce_and_spread)
+            lambda k: to_high(
+                4,
+                k,
+                column_sum.at[lax.rem(high_peer(k), owners)],
+                column_arrived.at[high_giver(k)],
+            ).wait_recv(),
+            high,
+        )
+        column_total[column_place()] = lax.fori_loop(
+            1,
+            high,
+            lambda k, t: t + column_arrived[high_giver(k)].astype(F32),
+            column_sum[column_place()].astype(F32),
+        ).astype(BF16)
+        each_peer(lambda k: column_spread(k).start(), high)
+
+    if_owner(reduce_column)
 
     def to_masters(b, c):
         put = put_rows(live[block_at(b), :], 0, masters)
         master_sum[...] += dot(put, picked[edges_at(b), :], (1, 0))
         return c
 
-    lax.fori_loop(0, blocks, to_masters, 0)
+    early = blocks // 2
+    lax.fori_loop(0, early, to_masters, 0)
+
+    each_peer(
+        guarded(
+            lambda k: to_high(
+                5,
+                k,
+                column_total.at[column_place()],
+                column_total.at[lax.rem(high_giver(k), owners)],
+            ).wait_recv(),
+            high_giver,
+        ),
+        high,
+    )
+    full[at_low] = column_total[...]
+
+    def spread(k):
+        return to_low(6, k, column_total, full.at[at_low])
+
+    each_peer(lambda k: spread(k).start(), low)
+    lax.fori_loop(early, blocks, to_masters, 0)
 
     each_peer(
         lambda k: copy(
@@ -279,32 +383,24 @@
     )
     hub_sum = lax.fori_loop(
         0,
-        parts,
-        lambda q, t: t + dot(hits(q), returned[rows_of(q), :], (1, 0)),
+        parts // batch,
+        lambda i, t: t + dot(hits[i], returned[batch_at(i), :], (1, 0)),
         master_sum[:HUBS, :],
     )
     out_ref[:HUBS, :] = hub_sum.astype(BF16)
     out_ref[HUBS:, :] = master_sum[HUBS:, :].astype(BF16)
 
-    each_peer(
-        guarded(
-            lambda k: copy(
-                4,
-                k,
-                summed.at[lax.rem(me, chunks)],
-                summed.at[lax.rem(giver(k), chunks)],
-            ).wait_recv(),
-            giver,
-        )
-    )
-    weights_ref[...] = summed[...]
+    each_peer(lambda k: to_low(6, k, column_total, full.at[low_giver(k)]).wait_recv(), low)
+    weights_ref[...] = full[...]
 
     exchange.wait_send()
     each_peer(lambda k: request(k).wait_send())
     each_peer(lambda k: reply(k).wait_send())
-    each_peer(guarded(lambda k: scatter(k).wait_send(), peer))
     each_peer(lambda k: give_back(k).wait_send())
-    each_peer(guarded(lambda k: spread(k).wait_send(), lambda k: me))
+    each_peer(lambda k: scatter(k).wait_send(), low)
+    each_peer(guarded(lambda k: scatter_high(k).wait_send(), high_peer), high)
+    if_owner(lambda: each_peer(lambda k: column_spread(k).wait_send(), high))
+    each_peer(lambda k: spread(k).wait_send(), low)
 
 
 def on_device(
@@ -327,19 +423,29 @@
     edges = edge_from.shape[0]
     full = w_self.shape[1]
     weight_rows = 2 * w_self.shape[0]
-    chunks = min(parts, weight_rows // 16)
-    chunk = weight_rows // chunks
-    block = min(edges, 1024 if masters + mirror_count <= 2048 else 256)
+    low = 2
+    while parts % (4 * low) == 0 and 4 * low * low <= parts:
+        low *= 2
+    low_rows = weight_rows // low
+    owners = min(parts // low, low_rows // 16)
+    chunk = low_rows // owners
+    batch = 8 if parts % 8 == 0 else 1
+    block = min(edges, 2048 if masters + mirror_count <= 2048 else 256)
     vmem = pl.BlockSpec(memory_space=pltpu.VMEM)
+    anywhere = pl.BlockSpec(memory_space=pl.ANY)
     input_grad, weights = pl.pallas_call(
         functools.partial(layer_kernel, parts, block),
         out_shape=(
             jax.ShapeDtypeStruct((masters, width), BF16),
-            jax.ShapeDtypeStruct((chunks, chunk, full), BF16),
+            jax.ShapeDtypeStruct((low, owners, chunk, full), BF16),
         ),
-        in_specs=[pl.BlockSpec(memory_space=pltpu.SMEM)] + [vmem] * 10,
+        in_specs=[pl.BlockSpec(memory_space=pltpu.SMEM)] + [vmem] * 2 + [anywhere] * 4 + [vmem] * 4,
         out_specs=(vmem, vmem),
         scratch_shapes=[
+            pltpu.VMEM(features.shape, BF16),
+            pltpu.VMEM(features.shape, BF16),
+            pltpu.VMEM(w_self.shape, BF16),
+            pltpu.VMEM(w_self.shape, BF16),
             pltpu.VMEM((2, masters, width), BF16),
             pltpu.VMEM((edges // LANES, LANES), jnp.int32),
             pltpu.VMEM((masters, width), BF16),
@@ -351,12 +457,17 @@
             pltpu.VMEM((mirror_count, width), F32),
             pltpu.VMEM((mirror_count, width), BF16),
             pltpu.VMEM((mirror_count, width), BF16),
-            pltpu.VMEM((chunks, chunk, full), BF16),
-            pltpu.VMEM((parts, chunk, full), BF16),
-            pltpu.VMEM((chunks, chunk, full), BF16),
+            pltpu.VMEM((parts // batch, HUBS, batch * slots), BF16),
+            pltpu.VMEM((low, low_rows, full), BF16),
+            pltpu.VMEM((low, low_rows, full), BF16),
+            pltpu.VMEM((owners, chunk, full), BF16),
+            pltpu.VMEM((parts // low, chunk, full), BF16),
+            pltpu.VMEM((owners, chunk, full), BF16),
+            pltpu.VMEM((low, owners, chunk, full), BF16),
+            pltpu.SemaphoreType.DMA((4,)),
             pltpu.SemaphoreType.DMA((2,)),
-            pltpu.SemaphoreType.DMA((5, parts)),
-            pltpu.SemaphoreType.DMA((5, parts)),
+            pltpu.SemaphoreType.DMA((7, parts)),
+            pltpu.SemaphoreType.DMA((7, parts)),
         ],
         compiler_params=pltpu.CompilerParams(
             collective_id=0, has_side_effects=True, vmem_limit_bytes=60 * 2**20

time: 56.9 us -> 53.6 us (0.942)
  Pallas kernels: 50.8 us -> 47.8 us
    pallas_call x1, Pallas kernels: 50.8 us -> 47.8 us  [on_device(): pl.pallas_call(functools.partial(layer_kernel, parts, block), out_shape=(...]
where the time goes in v3:
time: 53.6 us; the launch traced here: 53.4 us
  Pallas kernels  47.8 us (89%)
  local copies, waits for them, and re-layouts  4.34 us (8%)
  between operations  1.3 us (2%)
    pallas_call x1, Pallas kernels, on_device(): pl.pallas_call(functools.partial(layer_kernel, parts, block), out_shape=(...  47.8 us
    slice x1, local copies, waits for them, and re-layouts, on_device(): return (input_grad, weights[0], weights[1])  2.19 us
    unnamed x5, local copies, waits for them, and re-layouts  1.47 us

profile of v3, /device:TPU:0, one launch (start us, length us, event | category | flops | bytes accessed | tf_op | source)
XLA Modules:
  0.0 53.4 jit_solution(650494940048705512)
XLA Ops:
  1.3 0.0 copy-start.1
  1.3 0.7 %copy-done.1 = s32[512]{0:T(512)S(1)} copy-done((s32[512]{0:T(512)S(1)}, s32[512]{0:T(512)}, u32[]{:S(2)}) %copy-start.1) | copy-done | bytes 2072
  2.0 0.7 %reshape.26.wanted_ref = s32[16,1,32]{2,1,0:T(1,128)} reshape(s32[512]{0:T(512)S(1)} %copy-done.1) | data formatting | bytes 4096 | tf_op jit(solution)/shard_map/reshape | solution.py:485
  2.6 47.8 %shard_map.130 = (bf16[1024,256]{1,0:T(8,128)(2,1)}, bf16[4,4,32,512]{3,2,1,0:T(8,128)(2,1)}) custom-call(s32[1]{0:T(128)S(6)} %copy.15.limit_ref, bf16[1024,256]{1,0:T(8,128)(2,1)} %grad_ref.1, bf16[1024,256]{1,0:T(8,128)(2,1)} %pre_ref.1, bf16[1024,256]{1,0:T(8,128)(2,1)} %features_hbm.1, bf16[1024,256]{1,0:T(8,128)(2,1)} %mean_hbm.1, ...), custom_call_target="tpu_custom_call" | custom-call | tf_op jit(solution)/shard_map/pallas_call | solution.py:436
  50.4 0.0 copy-start
  50.4 2.2 %fusion = (f32[2,4,32,512]{3,2,1,0:T(8,128)}, f32[2,4,32,512]{3,2,1,0:T(8,128)}) fusion(bf16[4,4,32,512]{3,2,1,0:T(8,128)(2,1)} %get-tuple-element.6), kind=kLoop, calls=%fused_computation | loop fusion | bytes 2097152 | tf_op jit(solution)/shard_map/slice | solution.py:489
  52.6 0.0 copy-done
  52.6 0.8 %copy.16 = bf16[1024,256]{1,0:T(8,128)(2,1)} copy(bf16[1024,256]{1,0:T(8,128)(2,1)S(1)} %copy-done) | data formatting | bytes 1048576
Async XLA Ops:
  1.3 0.7 %copy-start.1 = (s32[512]{0:T(512)S(1)}, s32[512]{0:T(512)}, u32[]{:S(2)}) copy-start(s32[512]{0:T(512)} %param.20) | copy-start | bytes 6148
  50.4 2.2 %copy-start = (bf16[1024,256]{1,0:T(8,128)(2,1)S(1)}, bf16[1024,256]{1,0:T(8,128)(2,1)}, u32[]{:S(2)}) copy-start(bf16[1024,256]{1,0:T(8,128)(2,1)} %get-tuple-element.12) | copy-start | bytes 1572868

commit v4 on v3

--- a/solution.py
+++ b/solution.py
@@ -175,6 +175,47 @@
         device_id_type=MESH,
     ).wait_recv()
 
+    both = jnp.concatenate([cols[0], cols[1]], axis=1)
+    per_weight = low // 2
+    for i, operand in enumerate((features_ref, mean_ref)):
+        loads[1 + i].wait()
+        part = dot(operand[...], both, (0, 0)).astype(BF16)
+        for c in range(per_weight):
+            partial[i * per_weight + c] = part[c * low_rows : (c + 1) * low_rows, :]
+
+    def low_peer(k):
+        return lax.rem(at_low + k, low)
+
+    def low_giver(k):
+        return lax.rem(at_low + (low - k), low)
+
+    def high_peer(k):
+        return lax.rem(at_high + k, high)
+
+    def high_giver(k):
+        return lax.rem(at_high + (high - k), high)
+
+    def to_low(stage, k, src, dst):
+        return copy(stage, k, src, dst, at_high * low + low_peer(k))
+
+    def to_high(stage, k, src, dst):
+        return copy(stage, k, src, dst, high_peer(k) * low + at_low)
+
+    def guarded(act, owner):
+        if owners == high:
+            return act
+        return lambda k: pl.when(owner(k) < owners)(lambda: act(k))
+
+    def if_owner(act):
+        if owners == high:
+            act()
+        else:
+            pl.when(at_high < owners)(act)
+
+    def scatter(k):
+        return to_low(2, k, partial.at[low_peer(k)], arrived.at[at_low])
+
+    each_peer(lambda k: scatter(k).start(), low)
     loads[0].wait()
     neigh = dot(cols[0], w_neigh_ref[:, :width], (1, 1)) + dot(
         cols[1], w_neigh_ref[:, width:], (1, 1)
@@ -213,47 +254,6 @@
 
     each_peer(lambda k: reply(k).start())
 
-    both = jnp.concatenate([cols[0], cols[1]], axis=1)
-    per_weight = low // 2
-    for i, operand in enumerate((features_ref, mean_ref)):
-        loads[1 + i].wait()
-        part = dot(operand[...], both, (0, 0)).astype(BF16)
-        for c in range(per_weight):
-            partial[i * per_weight + c] = part[c * low_rows : (c + 1) * low_rows, :]
-
-    def low_peer(k):
-        return lax.rem(at_low + k, low)
-
-    def low_giver(k):
-        return lax.rem(at_low + (low - k), low)
-
-    def high_peer(k):
-        return lax.rem(at_high + k, high)
-
-    def high_giver(k):
-        return lax.rem(at_high + (high - k), high)
-
-    def to_low(stage, k, src, dst):
-        return copy(stage, k, src, dst, at_high * low + low_peer(k))
-
-    def to_high(stage, k, src, dst):
-        return copy(stage, k, src, dst, high_peer(k) * low + at_low)
-
-    def guarded(act, owner):
-        if owners == high:
-            return act
-        return lambda k: pl.when(owner(k) < owners)(lambda: act(k))
-
-    def if_owner(act):
-        if owners == high:
-            act()
-        else:
-            pl.when(at_high < owners)(act)
-
-    def scatter(k):
-        return to_low(2, k, partial.at[low_peer(k)], arrived.at[at_low])
-
-    each_peer(lambda k: scatter(k).start(), low)
     loads[3].wait()
     master_sum[...] = dot(cols[0], w_self_ref[:, :width], (1, 1)) + dot(
         cols[1], w_self_ref[:, width:], (1, 1)
@@ -310,20 +310,6 @@
         return c
 
     lax.fori_loop(0, blocks, from_mirrors, 0)
-
-    def to_mirrors(b, c):
-        put = put_rows(live[block_at(b), :], masters, mirror_count)
-        mirror_sum[...] += dot(put, picked[edges_at(b), :], (1, 0))
-        return c
-
-    lax.fori_loop(0, blocks, to_mirrors, 0)
-    returns[...] = mirror_sum[...].astype(BF16)
-    returned[rows_of(me), :] = returns[rows_of(me), :]
-
-    def give_back(k):
-        return copy(3, k, returns.at[rows_of(peer(k)), :], returned.at[rows_of(me), :])
-
-    each_peer(lambda k: give_back(k).start())
 
     def column_spread(k):
         return to_high(5, k, column_total.at[column_place()], column_total.at[column_place()])
@@ -348,13 +334,19 @@
 
     if_owner(reduce_column)
 
-    def to_masters(b, c):
-        put = put_rows(live[block_at(b), :], 0, masters)
-        master_sum[...] += dot(put, picked[edges_at(b), :], (1, 0))
+    def to_mirrors(b, c):
+        put = put_rows(live[block_at(b), :], masters, mirror_count)
+        mirror_sum[...] += dot(put, picked[edges_at(b), :], (1, 0))
         return c
 
-    early = blocks // 2
-    lax.fori_loop(0, early, to_masters, 0)
+    lax.fori_loop(0, blocks, to_mirrors, 0)
+    returns[...] = mirror_sum[...].astype(BF16)
+    returned[rows_of(me), :] = returns[rows_of(me), :]
+
+    def give_back(k):
+        return copy(3, k, returns.at[rows_of(peer(k)), :], returned.at[rows_of(me), :])
+
+    each_peer(lambda k: give_back(k).start())
 
     each_peer(
         guarded(
@@ -374,7 +366,13 @@
         return to_low(6, k, column_total, full.at[at_low])
 
     each_peer(lambda k: spread(k).start(), low)
-    lax.fori_loop(early, blocks, to_masters, 0)
+
+    def to_masters(b, c):
+        put = put_rows(live[block_at(b), :], 0, masters)
+        master_sum[...] += dot(put, picked[edges_at(b), :], (1, 0))
+        return c
+
+    lax.fori_loop(0, blocks, to_masters, 0)
 
     each_peer(
         lambda k: copy(

time: 53.6 us -> 47.2 us (0.88)
  Pallas kernels: 47.8 us -> 41.3 us
    pallas_call x1, Pallas kernels: 47.8 us -> 41.3 us  [on_device(): pl.pallas_call(functools.partial(layer_kernel, parts, block), out_shape=(...]
where the time goes in v4:
time: 47.2 us; the launch traced here: 47 us
  Pallas kernels  41.3 us (88%)
  local copies, waits for them, and re-layouts  4.34 us (9%)
  between operations  1.3 us (3%)
    pallas_call x1, Pallas kernels, on_device(): pl.pallas_call(functools.partial(layer_kernel, parts, block), out_shape=(...  41.3 us
    slice x1, local copies, waits for them, and re-layouts, on_device(): return (input_grad, weights[0], weights[1])  2.19 us
    unnamed x5, local copies, waits for them, and re-layouts  1.47 us

profile of v4, /device:TPU:0, one launch (start us, length us, event | category | flops | bytes accessed | tf_op | source)
XLA Modules:
  0.0 47.0 jit_solution(10122959114515865911)
XLA Ops:
  1.3 0.0 copy-start.1
  1.3 0.7 %copy-done.1 = s32[512]{0:T(512)S(1)} copy-done((s32[512]{0:T(512)S(1)}, s32[512]{0:T(512)}, u32[]{:S(2)}) %copy-start.1) | copy-done | bytes 2072
  2.0 0.7 %reshape.26.wanted_ref = s32[16,1,32]{2,1,0:T(1,128)} reshape(s32[512]{0:T(512)S(1)} %copy-done.1) | data formatting | bytes 4096 | tf_op jit(solution)/shard_map/reshape | solution.py:483
  2.6 41.3 %shard_map.130 = (bf16[1024,256]{1,0:T(8,128)(2,1)}, bf16[4,4,32,512]{3,2,1,0:T(8,128)(2,1)}) custom-call(s32[1]{0:T(128)S(6)} %copy.15.limit_ref, bf16[1024,256]{1,0:T(8,128)(2,1)} %grad_ref.1, bf16[1024,256]{1,0:T(8,128)(2,1)} %pre_ref.1, bf16[1024,256]{1,0:T(8,128)(2,1)} %features_hbm.1, bf16[1024,256]{1,0:T(8,128)(2,1)} %mean_hbm.1, ...), custom_call_target="tpu_custom_call" | custom-call | tf_op jit(solution)/shard_map/pallas_call | solution.py:434
  44.0 0.0 copy-start
  44.0 2.2 %fusion = (f32[2,4,32,512]{3,2,1,0:T(8,128)}, f32[2,4,32,512]{3,2,1,0:T(8,128)}) fusion(bf16[4,4,32,512]{3,2,1,0:T(8,128)(2,1)} %get-tuple-element.6), kind=kLoop, calls=%fused_computation | loop fusion | bytes 2097152 | tf_op jit(solution)/shard_map/slice | solution.py:487
  46.2 0.0 copy-done
  46.2 0.8 %copy.16 = bf16[1024,256]{1,0:T(8,128)(2,1)} copy(bf16[1024,256]{1,0:T(8,128)(2,1)S(1)} %copy-done) | data formatting | bytes 1048576
Async XLA Ops:
  1.3 0.7 %copy-start.1 = (s32[512]{0:T(512)S(1)}, s32[512]{0:T(512)}, u32[]{:S(2)}) copy-start(s32[512]{0:T(512)} %param.20) | copy-start | bytes 6148
  44.0 2.2 %copy-start = (bf16[1024,256]{1,0:T(8,128)(2,1)S(1)}, bf16[1024,256]{1,0:T(8,128)(2,1)}, u32[]{:S(2)}) copy-start(bf16[1024,256]{1,0:T(8,128)(2,1)} %get-tuple-element.12) | copy-start | bytes 1572868

commit v5 on v4

--- a/solution.py
+++ b/solution.py
@@ -166,6 +166,11 @@
         return copy(0, k, wanted_ref.at[peer(k)], asked.at[me])
 
     each_peer(lambda k: request(k).start())
+    def half_at(h):
+        return pl.ds(pl.multiple_of(h * width, width), width)
+
+    loads[0].wait()
+    own = dot(cols[half], w_neigh_ref[:, half_at(half)], (1, 1))
     pltpu.make_async_remote_copy(
         src_ref=cols.at[half],
         dst_ref=cols.at[partner],
@@ -216,10 +221,7 @@
         return to_low(2, k, partial.at[low_peer(k)], arrived.at[at_low])
 
     each_peer(lambda k: scatter(k).start(), low)
-    loads[0].wait()
-    neigh = dot(cols[0], w_neigh_ref[:, :width], (1, 1)) + dot(
-        cols[1], w_neigh_ref[:, width:], (1, 1)
-    )
+    neigh = own + dot(cols[partner], w_neigh_ref[:, half_at(partner)], (1, 1))
     for g in range(masters // LANES):
         at = slice(g * LANES, (g + 1) * LANES)
         degree = columns_of(degree_ref[g : g + 1, :]).astype(F32)
@@ -253,11 +255,6 @@
         return copy(1, k, replies.at[rows_of(peer(k)), :], mirrors.at[rows_of(me), :])
 
     each_peer(lambda k: reply(k).start())
-
-    loads[3].wait()
-    master_sum[...] = dot(cols[0], w_self_ref[:, :width], (1, 1)) + dot(
-        cols[1], w_self_ref[:, width:], (1, 1)
-    )
 
     def block_at(b):
         return pl.ds(pl.multiple_of(b * groups, groups), groups)
@@ -366,6 +363,11 @@
         return to_low(6, k, column_total, full.at[at_low])
 
     each_peer(lambda k: spread(k).start(), low)
+
+    loads[3].wait()
+    master_sum[...] = dot(cols[0], w_self_ref[:, :width], (1, 1)) + dot(
+        cols[1], w_self_ref[:, width:], (1, 1)
+    )
 
     def to_masters(b, c):
         put = put_rows(live[block_at(b), :], 0, masters)

time: 47.2 us -> 47.1 us (level)
  no operation moved by 1% of the time
where the time goes in v5:
time: 47.1 us; the launch traced here: 46.9 us
  Pallas kernels  41.3 us (88%)
  local copies, waits for them, and re-layouts  4.34 us (9%)
  between operations  1.3 us (3%)
    pallas_call x1, Pallas kernels, on_device(): pl.pallas_call(functools.partial(layer_kernel, parts, block), out_shape=(...  41.3 us
    slice x1, local copies, waits for them, and re-layouts, on_device(): return (input_grad, weights[0], weights[1])  2.19 us
    unnamed x5, local copies, waits for them, and re-layouts  1.47 us

profile of v5, /device:TPU:0, one launch (start us, length us, event | category | flops | bytes accessed | tf_op | source)
XLA Modules:
  0.0 46.9 jit_solution(4689413483223651674)
XLA Ops:
  1.3 0.0 copy-start.1
  1.3 0.7 %copy-done.1 = s32[512]{0:T(512)S(1)} copy-done((s32[512]{0:T(512)S(1)}, s32[512]{0:T(512)}, u32[]{:S(2)}) %copy-start.1) | copy-done | bytes 2072
  2.0 0.7 %reshape.26.wanted_ref = s32[16,1,32]{2,1,0:T(1,128)} reshape(s32[512]{0:T(512)S(1)} %copy-done.1) | data formatting | bytes 4096 | tf_op jit(solution)/shard_map/reshape | solution.py:485
  2.6 41.3 %shard_map.130 = (bf16[1024,256]{1,0:T(8,128)(2,1)}, bf16[4,4,32,512]{3,2,1,0:T(8,128)(2,1)}) custom-call(s32[1]{0:T(128)S(6)} %copy.15.limit_ref, bf16[1024,256]{1,0:T(8,128)(2,1)} %grad_ref.1, bf16[1024,256]{1,0:T(8,128)(2,1)} %pre_ref.1, bf16[1024,256]{1,0:T(8,128)(2,1)} %features_hbm.1, bf16[1024,256]{1,0:T(8,128)(2,1)} %mean_hbm.1, ...), custom_call_target="tpu_custom_call" | custom-call | tf_op jit(solution)/shard_map/pallas_call | solution.py:436
  44.0 0.0 copy-start
  44.0 2.2 %fusion = (f32[2,4,32,512]{3,2,1,0:T(8,128)}, f32[2,4,32,512]{3,2,1,0:T(8,128)}) fusion(bf16[4,4,32,512]{3,2,1,0:T(8,128)(2,1)} %get-tuple-element.6), kind=kLoop, calls=%fused_computation | loop fusion | bytes 2097152 | tf_op jit(solution)/shard_map/slice | solution.py:489
  46.2 0.0 copy-done
  46.2 0.8 %copy.16 = bf16[1024,256]{1,0:T(8,128)(2,1)} copy(bf16[1024,256]{1,0:T(8,128)(2,1)S(1)} %copy-done) | data formatting | bytes 1048576
Async XLA Ops:
  1.3 0.7 %copy-start.1 = (s32[512]{0:T(512)S(1)}, s32[512]{0:T(512)}, u32[]{:S(2)}) copy-start(s32[512]{0:T(512)} %param.20) | copy-start | bytes 6148
  44.0 2.2 %copy-start = (bf16[1024,256]{1,0:T(8,128)(2,1)S(1)}, bf16[1024,256]{1,0:T(8,128)(2,1)}, u32[]{:S(2)}) copy-start(bf16[1024,256]{1,0:T(8,128)(2,1)} %get-tuple-element.12) | copy-start | bytes 1572868
